TPU v7x, 32 devices: a whole 2x2x4 slice. The times are simulated.
32 devices in a mesh: ctx: 8 (over z, x), head: 4 (over y, core).
Axes of the slice: x: 2, y: 2, z: 4, core: 2. Of those that a mesh axis runs over, the one named last changes fastest.
Arguments:
- query: bfloat16 [8, 2, 128, 8192], P('ctx', None, 'head'), may hold values from -200 to 200
- keyval: bfloat16 [8, 2, 2, 128, 1024], P('ctx', None, None, 'head'), may hold values from -6 to 6
- doc_blocks: int32 [4], replicated, may hold values from 1 to 12, 16 in all
Outputs:
- attended: bfloat16 [8, 2, 128, 8192], P('ctx', None, 'head')
Inputs may be any that keep to these rules, and one draw needn't show every extreme that they name: `doc_blocks`: documents fill the sequence in order; the longest has exactly 12 blocks.
All inputs are finite; a program needn't handle non-finite values.
Results may differ from a plain program's by a relative error of at most 0.0038.
Values may be sent and summed in bfloat16 or wider, within the bound.
A program may use at most 64 MiB of HBM per device.

v0:
```python
import jax
import jax.numpy as jnp
from jax import lax
from jax.sharding import PartitionSpec as P

QUERY_HEADS = 64
KEY_VALUE_HEADS = 8
HEAD_WIDTH = 128
BLK = 128


def doc_index(positions, doc_ends):
    return jnp.sum((positions[:, None] >= doc_ends[None, :]).astype(jnp.int32), axis=1)


def local(query, keyval, doc_blocks):
    ctx_count = lax.axis_size("ctx")
    ctx_index = lax.axis_index("ctx")
    span_len = query.shape[2] * lax.axis_size("head")
    width_kv = keyval.shape[4]
    stacked = keyval.reshape(1, 4, keyval.shape[3], width_kv)
    query_heads, kv_heads = (
        lax.all_to_all(query, "head", split_axis=3, concat_axis=2, tiled=True),
        lax.all_to_all(stacked, "head", split_axis=3, concat_axis=2, tiled=True),
    )
    kv_local = kv_heads.shape[3] // HEAD_WIDTH
    heads_per_group = QUERY_HEADS // KEY_VALUE_HEADS
    kv_mine = kv_heads.reshape(1, 2, 2, span_len, kv_local * HEAD_WIDTH)
    row_count = 2 * span_len
    query_rows = query_heads.reshape(row_count, kv_local, heads_per_group, HEAD_WIDTH)
    offsets = jnp.arange(span_len, dtype=jnp.int32)
    query_pos = jnp.concatenate(
        [ctx_index * span_len + offsets, (2 * ctx_count - 1 - ctx_index) * span_len + offsets]
    )
    doc_ends = jnp.cumsum(doc_blocks) * BLK
    query_doc = doc_index(query_pos, doc_ends)
    scale_factor = HEAD_WIDTH ** (-0.5)
    initial = (
        jnp.full((kv_local, heads_per_group, row_count), -1e30, jnp.float32),
        jnp.zeros((kv_local, heads_per_group, row_count), jnp.float32),
        jnp.zeros((row_count, kv_local, heads_per_group, HEAD_WIDTH), jnp.float32),
    )
    gathered = lax.all_gather(kv_mine, "ctx", axis=0, tiled=True)
    running = initial
    count = gathered.shape[0]
    group_size = 4
    group_count = count // group_size
    grouped = gathered.reshape(group_count, group_size, 2, 2, span_len, kv_local * HEAD_WIDTH)
    firsts = jnp.arange(group_count, dtype=jnp.int32) * group_size

    def advance(state, payload):
        block_kv, lead_span = payload
        span_ids = lead_span + jnp.arange(group_size, dtype=jnp.int32)
        lower_pos = span_ids[:, None] * span_len + offsets[None, :]
        upper_pos = (2 * ctx_count - 1 - span_ids)[:, None] * span_len + offsets[None, :]
        key_pos = jnp.stack([lower_pos, upper_pos], axis=1).reshape(-1)
        key_row_block = block_kv[:, 0].reshape(-1, kv_local, HEAD_WIDTH)
        value_rows = block_kv[:, 1].reshape(-1, kv_local, HEAD_WIDTH)
        visible = (query_doc[:, None] == doc_index(key_pos, doc_ends)[None, :]) & (
            key_pos[None, :] <= query_pos[:, None]
        )
        row_max, totals, acc_sum = state
        scores = (
            jnp.einsum(
                "rgjd,kgd->gjrk", query_rows, key_row_block, preferred_element_type=jnp.float32
            )
            * scale_factor
        )
        scores = jnp.where(visible[None, None], scores, -1e30)
        new_max = jnp.maximum(row_max, jnp.max(scores, axis=-1))
        probs = jnp.where(visible[None, None], jnp.exp(scores - new_max[..., None]), 0.0)
        rescale = jnp.exp(row_max - new_max)
        totals = totals * rescale + jnp.sum(probs, axis=-1)
        added = jnp.einsum(
            "gjrk,kgd->rgjd",
            probs.astype(jnp.bfloat16),
            value_rows,
            preferred_element_type=jnp.float32,
        )
        acc_sum = acc_sum * jnp.moveaxis(rescale, 2, 0)[..., None] + added
        state = (new_max, totals, acc_sum)
        return (state, None)

    running, _ = lax.scan(advance, running, (grouped, firsts))
    row_max, totals, acc_sum = running
    result = (acc_sum / jnp.moveaxis(totals, 2, 0)[..., None]).astype(jnp.bfloat16)
    result = result.reshape(1, 2, span_len, kv_local * heads_per_group * HEAD_WIDTH)
    return lax.all_to_all(result, "head", split_axis=2, concat_axis=3, tiled=True)


def solution(mesh):
    placed = (P("ctx", None, "head", None), P("ctx", None, None, "head", None), P())
    return jax.shard_map(
        local, mesh=mesh, in_specs=placed, out_specs=P("ctx", None, "head", None), check_vma=False
    )
```

profile of v0, /device:TPU:0, one launch (start us, length us, event | category | flops | bytes accessed | tf_op | source)
XLA Modules:
  0.0 154.3 jit_solution(14284918072613798459)
XLA Ops:
  6.5 2.2 %copy.50 = bf16[1,2,2,32,1024]{3,2,1,4,0:T(2,128)(2,1)S(1)} copy(bf16[1,2,2,32,1024]{4,3,2,1,0:T(8,128)(2,1)} %param.6) | data formatting | bytes 524288 | tf_op args[1]
  9.7 10.1 %all_to_all.48 = bf16[4,2,16384]{2,1,0:T(2,128)(2,1)S(1)} all-to-all(bf16[4,2,16384]{2,1,0:T(2,128)(2,1)S(1)} %reshape.201), channel_id=1, replica_groups=mesh['ctx'=8,'head'=4] {'head'}, dimensions={0} | all-to-all | bytes 524288 | tf_op jit(solution)/shard_map/all_to_all | solution.py:24
  21.8 9.2 %copy.53 = bf16[1,2,32,8192]{2,1,0,3:T(2,128)(2,1)} copy(bf16[1,2,32,8192]{3,2,1,0:T(8,128)(2,1)} %param.5) | data formatting | bytes 2097152 | tf_op args[0]
  30.9 6.4 %reshape.203 = bf16[4,2,65536]{2,1,0:T(2,128)(2,1)} reshape(bf16[8192,1,2,32]{3,2,1,0:T(2,128)(2,1)} %bitcast.85) | data formatting | bytes 2097152
  37.3 3.5 %all-to-all-start.1 = ((bf16[4,2,65536]{2,1,0:T(2,128)(2,1)}), bf16[4,2,65536]{2,1,0:T(2,128)(2,1)S(1)}, u32[]{:S(2)}, u32[]{:S(2)}) async-start(bf16[4,2,65536]{2,1,0:T(2,128)(2,1)} %reshape.203), calls=%async_computation.1 | async-start | bytes 2097152 | tf_op jit(solution)/shard_map/all_to_all | solution.py:23
  41.2 14.1 %all-to-all-done.1 = bf16[4,2,65536]{2,1,0:T(2,128)(2,1)S(1)} async-done(((bf16[4,2,65536]{2,1,0:T(2,128)(2,1)}), bf16[4,2,65536]{2,1,0:T(2,128)(2,1)S(1)}, u32[]{:S(2)}, u32[]{:S(2)}) %all-to-all-start.1) | async-done | bytes 1048608 | tf_op jit(solution)/shard_map/all_to_all | solution.py:23
  55.3 3.5 %reshape.204 = bf16[8192,1,2,32]{3,2,1,0:T(2,128)(2,1)} reshape(bf16[4,2,65536]{2,1,0:T(2,128)(2,1)S(1)} %all-to-all-done.1) | data formatting | bytes 2097152
  58.8 9.0 %copy.54 = bf16[1,2,32,4,2048]{4,2,3,1,0:T(8,128)(2,1)S(1)} copy(bf16[1,2,32,4,2048]{2,1,4,3,0:T(2,128)(2,1)} %bitcast.84) | data formatting | bytes 2097152 | tf_op jit(solution)/shard_map/all_to_all | solution.py:23
  68.3 3.1 %all-gather.2.cloned.1.call-done = bf16[8,2,2,128,256]{4,3,2,1,0:T(8,128)(2,1)} async-done(((bf16[1,2,2,128,256]{4,3,2,1,0:T(8,128)(2,1)}), bf16[8,2,2,128,256]{4,3,2,1,0:T(8,128)(2,1)}) %all-gather.2.cloned.1.call-update) | async-done | bytes 2097168 | tf_op jit(solution)/shard_map/all_gather | solution.py:43
  71.3 52.6 %while.16 = (s32[]{:T(128)}, f32[2,8,256]{2,1,0:T(8,128)S(1)}, f32[2,8,256]{2,1,0:T(8,128)S(1)}, f32[256,2,8,128]{0,3,2,1:T(8,128)}, s32[256]{0:T(256)S(1)}, /*i...) while((s32[]{:T(128)}, f32[2,8,256]{2,1,0:T(8,128)S(1)}, ...), condition=%wide.region_6.7_spmd.clone.clone, body=%wide.region_2.6_spmd.clone.clone.sunk | while | flops 2204406784 | bytes 131365624 | solution.py:84
  73.2 1.3 copy_bitcast_fusion.2
  74.7 7.2 %fusion.33 = (f32[2,8,256]{2,1,0:T(8,128)S(1)}, f32[2,1024,256,8]{2,1,3,0:T(8,128)}) fusion(pred[256,1024]{0,1:T(8,128)(4,1)S(1)} %compare_and_fusion.2, bf16[256,2,8,128]{3,0,2,1:T(8,128)(2,1)S(1)} %get-tuple-element.319, bf16[1024,2,128,1]{2,1,0,3:T(2,128)(2,1)S(1)} %bitcast.83), kind=kOutput, calls=%fused_computation.3.clone.1 | convolution fusion | flops 1086320640 | bytes 18628608 | tf_op jit(solution)/shard_map/while/body/eval_jaxpr/rgjd,kgd->gjrk/dot_general | solution.py:64
  82.0 9.7 %bitcast_add_fusion.2 = f32[256,2,8,128]{0,3,2,1:T(8,128)} fusion(f32[256,2,8,128]{0,3,2,1:T(8,128)} %get-tuple-element.301, f32[2,1024,256,8]{2,1,3,0:T(8,128)} %get-tuple-element.283, f32[2,8,256]{2,1,0:T(8,128)S(1)} %get-tuple-element.311, pred[256,1024]{0,1:T(8,128)(4,1)S(1)} %compare_and_fusion.2, f32[256,2,8]{0,2,1:T(8,128)S(1)} %get-tuple-element.284, ...), kind=kOutput, calls=%fused_computation.8.clone.1 | convolution fusion | flops 1096286208 | bytes 21790720 | tf_op jit(solution)/shard_map/while/body/eval_jaxpr/gjrk,kgd->rgjd/dot_general | solution.py:74
  91.7 1.6 %copy-done = f32[2,1024,256,8]{2,1,3,0:T(8,128)S(1)} copy-done((f32[2,1024,256,8]{2,1,3,0:T(8,128)S(1)}, f32[2,1024,256,8]{2,1,3,0:T(8,128)}, u32[]{:S(2)}) %copy-start) | copy-done | bytes 16777240 | tf_op jit(solution)/shard_map/while
  93.3 4.0 %fusion.35 = f32[2,8,256]{2,1,0:T(8,128)S(1)} fusion(f32[2,1024,256,8]{2,1,3,0:T(8,128)S(1)} %copy-done, f32[2,8,256]{2,1,0:T(8,128)S(1)} %get-tuple-element.311, pred[256,1024]{0,1:T(8,128)(4,1)S(1)} %compare_and_fusion.2), kind=kLoop, calls=%fused_computation.5.clone.1 | loop fusion | flops 20967424 | bytes 17072128 | tf_op jit(solution)/shard_map/while/body/eval_jaxpr/reduce_sum | solution.py:73
  99.2 1.3 copy_bitcast_fusion.2
  100.7 7.2 %fusion.33 = (f32[2,8,256]{2,1,0:T(8,128)S(1)}, f32[2,1024,256,8]{2,1,3,0:T(8,128)}) fusion(pred[256,1024]{0,1:T(8,128)(4,1)S(1)} %compare_and_fusion.2, bf16[256,2,8,128]{3,0,2,1:T(8,128)(2,1)S(1)} %get-tuple-element.319, bf16[1024,2,128,1]{2,1,0,3:T(2,128)(2,1)S(1)} %bitcast.83), kind=kOutput, calls=%fused_computation.3.clone.1 | convolution fusion | flops 1086320640 | bytes 18628608 | tf_op jit(solution)/shard_map/while/body/eval_jaxpr/rgjd,kgd->gjrk/dot_general | solution.py:64
  108.1 10.3 %bitcast_add_fusion.2 = f32[256,2,8,128]{0,3,2,1:T(8,128)} fusion(f32[256,2,8,128]{0,3,2,1:T(8,128)} %get-tuple-element.301, f32[2,1024,256,8]{2,1,3,0:T(8,128)} %get-tuple-element.283, f32[2,8,256]{2,1,0:T(8,128)S(1)} %get-tuple-element.311, pred[256,1024]{0,1:T(8,128)(4,1)S(1)} %compare_and_fusion.2, f32[256,2,8]{0,2,1:T(8,128)S(1)} %get-tuple-element.284, ...), kind=kOutput, calls=%fused_computation.8.clone.1 | convolution fusion | flops 1096286208 | bytes 21790720 | tf_op jit(solution)/shard_map/while/body/eval_jaxpr/gjrk,kgd->rgjd/dot_general | solution.py:74
  118.3 1.6 %copy-done = f32[2,1024,256,8]{2,1,3,0:T(8,128)S(1)} copy-done((f32[2,1024,256,8]{2,1,3,0:T(8,128)S(1)}, f32[2,1024,256,8]{2,1,3,0:T(8,128)}, u32[]{:S(2)}) %copy-start) | copy-done | bytes 16777240 | tf_op jit(solution)/shard_map/while
  119.9 4.0 %fusion.35 = f32[2,8,256]{2,1,0:T(8,128)S(1)} fusion(f32[2,1024,256,8]{2,1,3,0:T(8,128)S(1)} %copy-done, f32[2,8,256]{2,1,0:T(8,128)S(1)} %get-tuple-element.311, pred[256,1024]{0,1:T(8,128)(4,1)S(1)} %compare_and_fusion.2), kind=kLoop, calls=%fused_computation.5.clone.1 | loop fusion | flops 20967424 | bytes 17072128 | tf_op jit(solution)/shard_map/while/body/eval_jaxpr/reduce_sum | solution.py:73
  124.0 1.8 %divide_convert_fusion = bf16[256,2,8,128]{0,3,2,1:T(8,128)(2,1)S(1)} fusion(f32[256,2,8,128]{0,3,2,1:T(8,128)} %get-tuple-element.66, f32[256,2,8]{0,2,1:T(8,128)S(1)} %bitcast.97), kind=kLoop, calls=%fused_computation.31 | loop fusion | flops 1048576 | bytes 3162112 | tf_op jit(solution)/shard_map/convert_element_type | solution.py:86
  126.1 3.1 %copy.58 = bf16[1,2,128,2048]{3,1,0,2:T(2,128)(2,1)S(1)} copy(bf16[1,2,128,2048]{2,1,3,0:T(2,128)(2,1)S(1)} %reshape.199) | data formatting | bytes 2097152 | tf_op jit(solution)/shard_map/reshape | solution.py:87
  129.1 17.0 %all_to_all.49 = bf16[1,2,128,2048]{3,1,0,2:T(2,128)(2,1)S(1)} all-to-all(bf16[1,2,128,2048]{3,1,0,2:T(2,128)(2,1)S(1)} %copy.58), channel_id=1, replica_groups=mesh['ctx'=8,'head'=4] {'head'}, dimensions={2} | all-to-all | bytes 2097152 | tf_op jit(solution)/shard_map/all_to_all | solution.py:88
  146.5 1.0 copy.73
  (49 shorter events, 8.7 us)
Async XLA Ops:
  6.5 34.4 %copy-start.1 = (s32[4]{0:T(128)S(1)}, s32[4]{0:T(128)}, u32[]{:S(2)}) copy-start(s32[4]{0:T(128)} %param.7) | copy-start | bytes 52
  6.5 64.8 %all-gather.2.cloned.1.call-start = ((), (), s32[]{:S(2)}) async-start(), calls=%async_computation.3 | async-start | bytes 2359296 | tf_op jit(solution)/shard_map/all_gather | solution.py:43
  37.3 17.9 %all-to-all-start.1 = ((bf16[4,2,65536]{2,1,0:T(2,128)(2,1)}), bf16[4,2,65536]{2,1,0:T(2,128)(2,1)S(1)}, u32[]{:S(2)}, u32[]{:S(2)}) async-start(bf16[4,2,65536]{2,1,0:T(2,128)(2,1)} %reshape.203), calls=%async_computation.1 | async-start | bytes 2097152 | tf_op jit(solution)/shard_map/all_to_all | solution.py:23
  82.0 11.3 %copy-start = (f32[2,1024,256,8]{2,1,3,0:T(8,128)S(1)}, f32[2,1024,256,8]{2,1,3,0:T(8,128)}, u32[]{:S(2)}) copy-start(f32[2,1024,256,8]{2,1,3,0:T(8,128)} %get-tuple-element.283) | copy-start | bytes 50331652 | tf_op jit(solution)/shard_map/while
  108.0 11.9 %copy-start = (f32[2,1024,256,8]{2,1,3,0:T(8,128)S(1)}, f32[2,1024,256,8]{2,1,3,0:T(8,128)}, u32[]{:S(2)}) copy-start(f32[2,1024,256,8]{2,1,3,0:T(8,128)} %get-tuple-element.283) | copy-start | bytes 50331652 | tf_op jit(solution)/shard_map/while
Sparse Core Ops, SparseCore 0:
  21.9 49.4 all-gather.1
where the time goes:
time: 156 us; the launch traced here: 154 us
  local copies, waits for them, and re-layouts  46 us (29%)
  matrix products  34.3 us (22%)
  blocking collectives  27 us (17%)
  waiting for transfers between devices  17.2 us (11%)
  between operations  13.5 us (9%)
  other arithmetic  12.5 us (8%)
  starting transfers between devices  3.52 us (2%)
    unnamed x10, local copies, waits for them, and re-layouts  23.3 us
    dot_general x2, matrix products, advance(): jnp.einsum('gjrk,kgd->rgjd', probs.astype(jnp.bfloat16), value_rows, pref...  20 us
    all_to_all x1, blocking collectives, local(): lax.all_to_all(result, 'head', split_axis=2, concat_axis=3, tiled=True)  17 us
    dot_general x2, matrix products, advance(): jnp.einsum('rgjd,kgd->gjrk', query_rows, key_row_block, preferred_element...  14.3 us
    all_to_all x1, waiting for transfers between devices, local(): lax.all_to_all(query, 'head', split_axis=3, concat_axis=2, tiled=True)  14.1 us
    all_to_all x1, blocking collectives, local(): lax.all_to_all(stacked, 'head', split_axis=3, concat_axis=2, tiled=True)  10.1 us
    all_to_all x1, local copies, waits for them, and re-layouts, local(): lax.all_to_all(query, 'head', split_axis=3, concat_axis=2, tiled=True)  8.96 us
    reduce_sum x2, other arithmetic, advance(): totals = totals * rescale + jnp.sum(probs, axis=-1)  7.97 us
  transfers between devices with their start and end apart: 2, of which 2 were waited for; matrix products, arithmetic and copies ran while one was open for 19% of the time, Pallas kernels for 0%

commit v1 on v0

--- a/solution.py
+++ b/solution.py
@@ -85,7 +85,10 @@
     row_max, totals, acc_sum = running
     result = (acc_sum / jnp.moveaxis(totals, 2, 0)[..., None]).astype(jnp.bfloat16)
     result = result.reshape(1, 2, span_len, kv_local * heads_per_group * HEAD_WIDTH)
-    return lax.all_to_all(result, "head", split_axis=2, concat_axis=3, tiled=True)
+    return jnp.concatenate(
+        lax.all_to_all(jnp.stack(jnp.split(result, lax.axis_size("head"), axis=2)), "head", 0, 0),
+        axis=3,
+    )
 
 
 def solution(mesh):

time: 156 us -> 163 us (1.045)
  local copies, waits for them, and re-layouts: 46 us -> 53.6 us
    unnamed x10 -> x14, local copies, waits for them, and re-layouts: 23.3 us -> 29.3 us
    split x0 -> x1, local copies, waits for them, and re-layouts: none -> 4.92 us  [local(): jnp.split(result, lax.axis_size('head'), axis=2)]
    reshape x2 -> x1, local copies, waits for them, and re-layouts: 3.35 us -> 0.29 us  [local(): result.reshape(1, 2, span_len, kv_local * heads_per_group * HEAD_WIDTH)]
  transfers between devices with their start and end apart: 2 -> 2, of which waited for: 2 -> 2; matrix products, arithmetic and copies ran while one was open for 19% -> 18% of each run, Pallas kernels for 0% -> 0%
where the time goes in v1:
time: 163 us; the launch traced here: 162 us
  local copies, waits for them, and re-layouts  53.6 us (33%)
  matrix products  34.3 us (21%)
  blocking collectives  27 us (17%)
  waiting for transfers between devices  17 us (10%)
  between operations  13.6 us (8%)
  other arithmetic  12.7 us (8%)
  starting transfers between devices  3.7 us (2%)
    unnamed x14, local copies, waits for them, and re-layouts  29.3 us
    dot_general x2, matrix products, advance(): jnp.einsum('gjrk,kgd->rgjd', probs.astype(jnp.bfloat16), value_rows, pref...  20 us
    all_to_all x1, blocking collectives, local(): lax.all_to_all(jnp.stack(jnp.split(result, lax.axis_size('head'), axis=2)...  17 us
    dot_general x2, matrix products, advance(): jnp.einsum('rgjd,kgd->gjrk', query_rows, key_row_block, preferred_element...  14.3 us
    all_to_all x1, waiting for transfers between devices, local(): lax.all_to_all(query, 'head', split_axis=3, concat_axis=2, tiled=True)  13.9 us
    all_to_all x1, blocking collectives, local(): lax.all_to_all(stacked, 'head', split_axis=3, concat_axis=2, tiled=True)  10.1 us
    all_to_all x1, local copies, waits for them, and re-layouts, local(): lax.all_to_all(query, 'head', split_axis=3, concat_axis=2, tiled=True)  8.96 us
    reduce_sum x2, other arithmetic, advance(): totals = totals * rescale + jnp.sum(probs, axis=-1)  7.97 us
  transfers between devices with their start and end apart: 2, of which 2 were waited for; matrix products, arithmetic and copies ran while one was open for 18% of the time, Pallas kernels for 0%

profile of v1, /device:TPU:0, one launch (start us, length us, event | category | flops | bytes accessed | tf_op | source)
XLA Modules:
  0.0 162.0 jit_solution(12756936302469013470)
XLA Ops:
  6.5 2.2 %copy.40 = bf16[1,2,2,32,1024]{3,2,1,4,0:T(2,128)(2,1)S(1)} copy(bf16[1,2,2,32,1024]{4,3,2,1,0:T(8,128)(2,1)} %param.6) | data formatting | bytes 524288 | tf_op args[1]
  9.7 10.1 %all_to_all.35 = bf16[4,2,16384]{2,1,0:T(2,128)(2,1)S(1)} all-to-all(bf16[4,2,16384]{2,1,0:T(2,128)(2,1)S(1)} %reshape.209), channel_id=1, replica_groups=mesh['ctx'=8,'head'=4] {'head'}, dimensions={0} | all-to-all | bytes 524288 | tf_op jit(solution)/shard_map/all_to_all | solution.py:24
  21.8 9.2 %copy.43 = bf16[1,2,32,8192]{2,1,0,3:T(2,128)(2,1)} copy(bf16[1,2,32,8192]{3,2,1,0:T(8,128)(2,1)} %param.5) | data formatting | bytes 2097152 | tf_op args[0]
  30.9 6.4 %reshape.211 = bf16[4,2,65536]{2,1,0:T(2,128)(2,1)} reshape(bf16[8192,1,2,32]{3,2,1,0:T(2,128)(2,1)} %bitcast.87) | data formatting | bytes 2097152
  37.3 3.7 %all-to-all-start.1 = ((bf16[4,2,65536]{2,1,0:T(2,128)(2,1)}), bf16[4,2,65536]{2,1,0:T(2,128)(2,1)S(1)}, u32[]{:S(2)}, u32[]{:S(2)}) async-start(bf16[4,2,65536]{2,1,0:T(2,128)(2,1)} %reshape.211), calls=%async_computation.1 | async-start | bytes 2097152 | tf_op jit(solution)/shard_map/all_to_all | solution.py:23
  41.4 13.9 %all-to-all-done.1 = bf16[4,2,65536]{2,1,0:T(2,128)(2,1)S(1)} async-done(((bf16[4,2,65536]{2,1,0:T(2,128)(2,1)}), bf16[4,2,65536]{2,1,0:T(2,128)(2,1)S(1)}, u32[]{:S(2)}, u32[]{:S(2)}) %all-to-all-start.1) | async-done | bytes 1048608 | tf_op jit(solution)/shard_map/all_to_all | solution.py:23
  55.3 3.5 %reshape.212 = bf16[8192,1,2,32]{3,2,1,0:T(2,128)(2,1)} reshape(bf16[4,2,65536]{2,1,0:T(2,128)(2,1)S(1)} %all-to-all-done.1) | data formatting | bytes 2097152
  58.8 9.0 %copy.44 = bf16[1,2,32,4,2048]{4,2,3,1,0:T(8,128)(2,1)S(1)} copy(bf16[1,2,32,4,2048]{2,1,4,3,0:T(2,128)(2,1)} %bitcast.86) | data formatting | bytes 2097152 | tf_op jit(solution)/shard_map/all_to_all | solution.py:23
  68.3 3.1 %all-gather.2.cloned.1.call-done = bf16[8,2,2,128,256]{4,3,2,1,0:T(8,128)(2,1)} async-done(((bf16[1,2,2,128,256]{4,3,2,1,0:T(8,128)(2,1)}), bf16[8,2,2,128,256]{4,3,2,1,0:T(8,128)(2,1)}) %all-gather.2.cloned.1.call-update) | async-done | bytes 2097168 | tf_op jit(solution)/shard_map/all_gather | solution.py:43
  71.3 52.6 %while.16 = (s32[]{:T(128)}, f32[2,8,256]{2,1,0:T(8,128)S(1)}, f32[2,8,256]{2,1,0:T(8,128)S(1)}, f32[256,2,8,128]{0,3,2,1:T(8,128)}, s32[256]{0:T(256)S(1)}, /*i...) while((s32[]{:T(128)}, f32[2,8,256]{2,1,0:T(8,128)S(1)}, ...), condition=%wide.region_6.7_spmd.clone.clone, body=%wide.region_2.6_spmd.clone.clone.sunk | while | flops 2204406784 | bytes 131365624 | solution.py:84
  73.2 1.3 copy_bitcast_fusion.2
  74.7 7.2 %fusion.34 = (f32[2,8,256]{2,1,0:T(8,128)S(1)}, f32[2,1024,256,8]{2,1,3,0:T(8,128)}) fusion(pred[256,1024]{0,1:T(8,128)(4,1)S(1)} %compare_and_fusion.2, bf16[256,2,8,128]{3,0,2,1:T(8,128)(2,1)S(1)} %get-tuple-element.313, bf16[1024,2,128,1]{2,1,0,3:T(2,128)(2,1)S(1)} %bitcast.85), kind=kOutput, calls=%fused_computation.3.clone.1 | convolution fusion | flops 1086320640 | bytes 18628608 | tf_op jit(solution)/shard_map/while/body/eval_jaxpr/rgjd,kgd->gjrk/dot_general | solution.py:64
  82.0 9.7 %bitcast_add_fusion.2 = f32[256,2,8,128]{0,3,2,1:T(8,128)} fusion(f32[256,2,8,128]{0,3,2,1:T(8,128)} %get-tuple-element.295, f32[2,1024,256,8]{2,1,3,0:T(8,128)} %get-tuple-element.277, f32[2,8,256]{2,1,0:T(8,128)S(1)} %get-tuple-element.305, pred[256,1024]{0,1:T(8,128)(4,1)S(1)} %compare_and_fusion.2, f32[256,2,8]{0,2,1:T(8,128)S(1)} %get-tuple-element.278, ...), kind=kOutput, calls=%fused_computation.8.clone.1 | convolution fusion | flops 1096286208 | bytes 21790720 | tf_op jit(solution)/shard_map/while/body/eval_jaxpr/gjrk,kgd->rgjd/dot_general | solution.py:74
  91.7 1.6 copy-done
  93.3 4.0 %fusion.36 = f32[2,8,256]{2,1,0:T(8,128)S(1)} fusion(f32[2,1024,256,8]{2,1,3,0:T(8,128)S(1)} %copy-done, f32[2,8,256]{2,1,0:T(8,128)S(1)} %get-tuple-element.305, pred[256,1024]{0,1:T(8,128)(4,1)S(1)} %compare_and_fusion.2), kind=kLoop, calls=%fused_computation.5.clone.1 | loop fusion | flops 20967424 | bytes 17072128 | tf_op jit(solution)/shard_map/while/body/eval_jaxpr/reduce_sum | solution.py:73
  100.7 7.2 %fusion.34 = (f32[2,8,256]{2,1,0:T(8,128)S(1)}, f32[2,1024,256,8]{2,1,3,0:T(8,128)}) fusion(pred[256,1024]{0,1:T(8,128)(4,1)S(1)} %compare_and_fusion.2, bf16[256,2,8,128]{3,0,2,1:T(8,128)(2,1)S(1)} %get-tuple-element.313, bf16[1024,2,128,1]{2,1,0,3:T(2,128)(2,1)S(1)} %bitcast.85), kind=kOutput, calls=%fused_computation.3.clone.1 | convolution fusion | flops 1086320640 | bytes 18628608 | tf_op jit(solution)/shard_map/while/body/eval_jaxpr/rgjd,kgd->gjrk/dot_general | solution.py:64
  108.0 10.3 %bitcast_add_fusion.2 = f32[256,2,8,128]{0,3,2,1:T(8,128)} fusion(f32[256,2,8,128]{0,3,2,1:T(8,128)} %get-tuple-element.295, f32[2,1024,256,8]{2,1,3,0:T(8,128)} %get-tuple-element.277, f32[2,8,256]{2,1,0:T(8,128)S(1)} %get-tuple-element.305, pred[256,1024]{0,1:T(8,128)(4,1)S(1)} %compare_and_fusion.2, f32[256,2,8]{0,2,1:T(8,128)S(1)} %get-tuple-element.278, ...), kind=kOutput, calls=%fused_computation.8.clone.1 | convolution fusion | flops 1096286208 | bytes 21790720 | tf_op jit(solution)/shard_map/while/body/eval_jaxpr/gjrk,kgd->rgjd/dot_general | solution.py:74
  118.3 1.6 copy-done
  119.9 4.0 %fusion.36 = f32[2,8,256]{2,1,0:T(8,128)S(1)} fusion(f32[2,1024,256,8]{2,1,3,0:T(8,128)S(1)} %copy-done, f32[2,8,256]{2,1,0:T(8,128)S(1)} %get-tuple-element.305, pred[256,1024]{0,1:T(8,128)(4,1)S(1)} %compare_and_fusion.2), kind=kLoop, calls=%fused_computation.5.clone.1 | loop fusion | flops 20967424 | bytes 17072128 | tf_op jit(solution)/shard_map/while/body/eval_jaxpr/reduce_sum | solution.py:73
  124.0 1.8 %divide_convert_fusion = bf16[256,2,8,128]{0,3,2,1:T(8,128)(2,1)S(1)} fusion(f32[256,2,8,128]{0,3,2,1:T(8,128)} %get-tuple-element.66, f32[256,2,8]{0,2,1:T(8,128)S(1)} %bitcast.103), kind=kLoop, calls=%fused_computation.31 | loop fusion | flops 1048576 | bytes 3162112 | tf_op jit(solution)/shard_map/convert_element_type | solution.py:86
  126.1 4.9 %fusion.20 = (bf16[1,2,32,2048]{2,1,3,0:T(2,128)(2,1)}, bf16[1,2,32,2048]{2,1,3,0:T(2,128)(2,1)S(1)}, bf16[1,2,32,2048]{2,1,3,0:T(2,128)(2,1)}, bf16[1,2,32,2048]{2,1,3,0:T(2,128)(2,1)S(1)}) fusion(bf16[1,2,128,2048]{2,1,3,0:T(2,128)(2,1)S(1)} %reshape.207), kind=kLoop, calls=%fused_computation.40 | loop fusion | bytes 2097152 | tf_op jit(solution)/shard_map/split | solution.py:89
  131.0 2.3 %copy.60 = bf16[1,2,32,2048]{3,2,1,0:T(8,128)(2,1)S(1)} copy(bf16[1,2,32,2048]{2,1,3,0:T(2,128)(2,1)} %get-tuple-element.197) | data formatting | bytes 524288
  133.3 2.3 %copy.61 = bf16[1,2,32,2048]{3,2,1,0:T(8,128)(2,1)S(1)} copy(bf16[1,2,32,2048]{2,1,3,0:T(2,128)(2,1)} %get-tuple-element.199) | data formatting | bytes 524288
  137.2 17.0 %all_to_all.36 = bf16[4,1,2,32,2048]{4,3,2,1,0:T(8,128)(2,1)S(1)} all-to-all(bf16[4,1,2,32,2048]{4,3,2,1,0:T(8,128)(2,1)S(1)} %pad_maximum_fusion), channel_id=1, replica_groups=mesh['ctx'=8,'head'=4] {'head'}, dimensions={0} | all-to-all | bytes 2097152 | tf_op jit(solution)/shard_map/all_to_all | solution.py:89
  (53 shorter events, 12.2 us)
Async XLA Ops:
  6.5 34.5 %copy-start.1 = (s32[4]{0:T(128)S(1)}, s32[4]{0:T(128)}, u32[]{:S(2)}) copy-start(s32[4]{0:T(128)} %param.7) | copy-start | bytes 52
  6.5 64.8 %all-gather.2.cloned.1.call-start = ((), (), s32[]{:S(2)}) async-start(), calls=%async_computation.3 | async-start | bytes 2359296 | tf_op jit(solution)/shard_map/all_gather | solution.py:43
  37.3 17.9 %all-to-all-start.1 = ((bf16[4,2,65536]{2,1,0:T(2,128)(2,1)}), bf16[4,2,65536]{2,1,0:T(2,128)(2,1)S(1)}, u32[]{:S(2)}, u32[]{:S(2)}) async-start(bf16[4,2,65536]{2,1,0:T(2,128)(2,1)} %reshape.211), calls=%async_computation.1 | async-start | bytes 2097152 | tf_op jit(solution)/shard_map/all_to_all | solution.py:23
  82.0 11.3 %copy-start = (f32[2,1024,256,8]{2,1,3,0:T(8,128)S(1)}, f32[2,1024,256,8]{2,1,3,0:T(8,128)}, u32[]{:S(2)}) copy-start(f32[2,1024,256,8]{2,1,3,0:T(8,128)} %get-tuple-element.277) | copy-start | bytes 50331652 | tf_op jit(solution)/shard_map/while
  108.0 11.9 %copy-start = (f32[2,1024,256,8]{2,1,3,0:T(8,128)S(1)}, f32[2,1024,256,8]{2,1,3,0:T(8,128)}, u32[]{:S(2)}) copy-start(f32[2,1024,256,8]{2,1,3,0:T(8,128)} %get-tuple-element.277) | copy-start | bytes 50331652 | tf_op jit(solution)/shard_map/while
Sparse Core Ops, SparseCore 0:
  21.9 49.4 all-gather.1
